TPU v7x, 256 devices: a whole 4x4x8 slice. The times are simulated.
256 devices in a mesh: ha: 8 (over x, y_lo), wa: 32 (over z, y_hi, core).
Axes of the slice: x: 4, y: 4 (y_hi: 2, y_lo: 2; y = y_hi * 2 + y_lo), z: 8, core: 2. Of those that a mesh axis runs over, the one named last changes fastest.
Arguments:
- tokens: bfloat16 [4, 64, 256, 1536], P(None, 'ha', 'wa'), may hold values from -6 to 6
- shift: float32 [1536], replicated, may hold values from -3 to 3
- scale: float32 [1536], replicated, may hold values from -3 to 3
- gate: float32 [1536], replicated, may hold values from -4 to 4
- qkv_weight: bfloat16 [1536, 4608], P('wa'), may hold values from -0.17860863 to 0.17860863
- out_weight: bfloat16 [1536, 1536], P('wa'), may hold values from -0.15625 to 0.15625
- q_gain: float32 [128], replicated, may hold values from 1.4 to 6.5
- k_gain: float32 [128], replicated, may hold values from 1.4 to 6.5
Outputs:
- update: bfloat16 [4, 64, 256, 1536], P(None, 'ha', 'wa')
All inputs are finite; a program needn't handle non-finite values.
Results may differ from a plain program's by a relative error of at most 0.009.
The roundings to bfloat16 on the way count: a program that leaves them out, or rounds other values in their place, can miss the bound.
Values may be sent and summed in bfloat16 or wider, within the bound.
No kernel may reach another device: no remote copies, remote signals or barrier semaphores. Data moves between devices by JAX's collectives and lax.ppermute only.
A program may use at most 128 MiB of HBM per device.

v0:
```python
import jax
import jax.numpy as jnp
from jax import lax
from jax.sharding import PartitionSpec as P

HEADS = 12
HD = 128
TILE_T = 4


def padded(x, sides, width):
    for axis, dim in sides:
        peers, length = (lax.axis_size(axis), x.shape[dim])
        up = [(i, (i + 1) % peers) for i in range(peers - 1)]
        down = [(j, i) for i, j in up]
        last = lax.slice_in_dim(x, length - width, length, axis=dim)
        initial = lax.slice_in_dim(x, 0, width, axis=dim)
        before = lax.ppermute(last, axis, up)
        after = lax.ppermute(initial, axis, down)
        x = jnp.concatenate([before, x, after], axis=dim)
    return x


def add_rows(left, piece):
    return jnp.dot(left, piece, preferred_element_type=jnp.float32)


def per_head_norm(raw, gain):
    return (raw * lax.rsqrt(jnp.mean(raw * raw, axis=-1, keepdims=True) + 1e-06) * gain).astype(
        jnp.bfloat16
    )


def shards(tokens, shift, scale, gate, qkv_weight, out_weight, q_gain, k_gain):
    frame_list, tile_h, tile_w, width = tokens.shape
    count = frame_list * tile_h * tile_w
    inner = HEADS * HD
    groups = frame_list // TILE_T
    tall = lax.axis_size("ha")
    wide = lax.axis_size("wa")
    flat = tokens.reshape(count, width).astype(jnp.float32)
    mean = jnp.mean(flat, axis=-1, keepdims=True)
    centred = flat - mean
    var = jnp.mean(centred * centred, axis=-1, keepdims=True)
    normed = centred / jnp.sqrt(var + 1e-06)
    modulated = (normed * (1.0 + scale) + shift).astype(jnp.bfloat16)
    projected = add_rows(modulated, lax.all_gather(qkv_weight, "wa", axis=0, tiled=True))
    query = per_head_norm(projected[:, :inner].reshape(count, HEADS, HD), q_gain)
    key = per_head_norm(projected[:, inner : 2 * inner].reshape(count, HEADS, HD), k_gain)
    value = projected[:, 2 * inner :].astype(jnp.bfloat16)
    both = jnp.concatenate(
        [
            key.reshape(frame_list, tile_h, tile_w, inner),
            value.reshape(frame_list, tile_h, tile_w, inner),
        ],
        axis=-1,
    )
    window = padded(both, (("ha", 1), ("wa", 2)), tile_h)
    rows = lax.axis_index("ha") * tile_h - tile_h + jnp.arange(3 * tile_h, dtype=jnp.int32)
    cols = lax.axis_index("wa") * tile_w - tile_w + jnp.arange(3 * tile_w, dtype=jnp.int32)
    rows_ok = (rows >= 0) & (rows < tile_h * tall)
    cols_ok = (cols >= 0) & (cols < tile_w * wide)
    valid = jnp.broadcast_to(
        rows_ok[:, None] & cols_ok[None, :], (TILE_T, 3 * tile_h, 3 * tile_w)
    ).reshape(-1)
    window = window.reshape(groups, -1, 2 * inner)
    keys = window[:, :, :inner].reshape(groups, -1, HEADS, HD)
    values = window[:, :, inner:].reshape(groups, -1, HEADS, HD)
    queries = query.reshape(groups, -1, HEADS, HD)
    inv_root = 1.0 / jnp.sqrt(jnp.float32(HD))

    def one_head(head):
        query_head_rows = lax.dynamic_index_in_dim(queries, head, 2, keepdims=False)
        key_head_rows = lax.dynamic_index_in_dim(keys, head, 2, keepdims=False)
        value_head_rows = lax.dynamic_index_in_dim(values, head, 2, keepdims=False)
        scores = (
            jnp.einsum(
                "nur,ncr->nuc", query_head_rows, key_head_rows, preferred_element_type=jnp.float32
            )
            * inv_root
        )
        scores = jnp.where(valid[None, None, :], scores, -jnp.inf)
        top = jnp.max(scores, axis=-1, keepdims=True)
        expo = jnp.exp(scores - top)
        total = jnp.sum(expo, axis=-1, keepdims=True)
        probability_rows = expo.astype(jnp.bfloat16)
        summed_output = jnp.einsum(
            "ypi,yif->ypf", probability_rows, value_head_rows, preferred_element_type=jnp.float32
        )
        return summed_output / total

    per_head = lax.map(one_head, jnp.arange(HEADS, dtype=jnp.int32))
    attended = jnp.transpose(per_head, (1, 2, 0, 3)).reshape(count, inner).astype(jnp.bfloat16)
    output = add_rows(attended, lax.all_gather(out_weight, "wa", axis=0, tiled=True))
    return (gate * output).astype(jnp.bfloat16).reshape(frame_list, tile_h, tile_w, width)


def solution(mesh):
    return jax.shard_map(
        shards,
        mesh=mesh,
        in_specs=(P(None, "ha", "wa", None), P(), P(), P(), P("wa", None), P("wa", None), P(), P()),
        out_specs=P(None, "ha", "wa", None),
        check_vma=False,
    )
```

profile of v0, /device:TPU:28, one launch (start us, length us, event | category | flops | bytes accessed | tf_op | source)
XLA Modules:
  0.0 474.7 jit_solution(12902752711311697447)
XLA Ops:
  12.1 123.9 %all-gather.3.cloned.1.call-done = bf16[1536,4608]{1,0:T(8,128)(2,1)} async-done(((bf16[48,4608]{1,0:T(8,128)(2,1)}), bf16[1536,4608]{1,0:T(8,128)(2,1)}) %all-gather.3.cloned.1.call-update) | async-done | bytes 14155792 | tf_op jit(solution)/shard_map/all_gather | solution.py:47
  136.0 7.0 %fusion.29 = f32[256,4608]{1,0:T(8,128)S(1)} fusion(bf16[256,1536]{1,0:T(8,128)(2,1)S(1)} %fusion.26, bf16[1536,4608]{1,0:T(8,128)(2,1)} %all-gather.3.cloned.1.call-done), kind=kOutput, calls=%fused_computation.47 | convolution fusion | flops 3623878656 | bytes 19660800 | tf_op jit(solution)/shard_map/dot_general | solution.py:25
  143.1 2.5 slice_multiply_fusion
  150.9 2.2 multiply_convert_fusion
  153.3 1.9 collective-permute-start.1
  155.2 4.8 %collective-permute-start = (bf16[4,8,8,3072]{3,2,1,0:T(8,128)(2,1)S(1)}, bf16[4,8,8,3072]{3,2,1,0:T(8,128)(2,1)S(1)}, u32[]{:S(2)}, u32[]{:S(2)}) collective-permute-start(bf16[4,8,8,3072]{3,2,1,0:T(8,128)(2,1)S(1)} %pad_maximum_fusion.2), channel_id=1, source_target_pairs={{0,32},{32,64},{64,96},{96,128},{128,160},{160,192},{192,224},{1,3... | collective-permute-start | bytes 4718600 | tf_op jit(solution)/shard_map/ppermute | solution.py:18
  160.1 63.2 %collective-permute-done.1 = bf16[4,8,8,3072]{3,2,1,0:T(8,128)(2,1)S(1)} collective-permute-done((bf16[4,8,8,3072]{3,2,1,0:T(8,128)(2,1)S(1)}, bf16[4,8,8,3072]{3,2,1,0:T(8,128)(2,1)S(1)}, u32[]{:S(2)}, u32[]{:S(2)}) %collective-permute-start.1) | collective-permute-done | bytes 1572896 | tf_op jit(solution)/shard_map/ppermute | solution.py:19
  223.3 3.1 collective-permute-done
  226.4 2.7 pad_maximum_fusion.1
  229.1 3.6 collective-permute-start.3
  232.7 1.9 collective-permute-start.2
  234.8 3.0 copy.9
  237.8 3.0 copy.10
  242.4 2.7 multiply_convert_fusion.1
  245.1 41.1 %collective-permute-done.3 = bf16[4,24,8,3072]{3,2,1,0:T(8,128)(2,1)} collective-permute-done((bf16[4,24,8,3072]{3,2,1,0:T(8,128)(2,1)}, bf16[4,24,8,3072]{3,2,1,0:T(8,128)(2,1)}, u32[]{:S(2)}, u32[]{:S(2)}) %collective-permute-start.3) | collective-permute-done | bytes 4718624 | tf_op jit(solution)/shard_map/ppermute | solution.py:19
  286.2 66.0 %collective-permute-done.2 = bf16[4,24,8,3072]{3,2,1,0:T(8,128)(2,1)} collective-permute-done((bf16[4,24,8,3072]{3,2,1,0:T(8,128)(2,1)}, bf16[4,24,8,3072]{3,2,1,0:T(8,128)(2,1)}, u32[]{:S(2)}, u32[]{:S(2)}) %collective-permute-start.2) | collective-permute-done | bytes 4718624 | tf_op jit(solution)/shard_map/ppermute | solution.py:18
  352.2 6.8 %pad_maximum_fusion = bf16[4,24,24,3072]{3,2,1,0:T(8,128)(2,1)S(1)} fusion(bf16[4,24,8,3072]{3,2,1,0:T(8,128)(2,1)} %collective-permute-done.3, bf16[4,8,8,3072]{3,2,1,0:T(8,128)(2,1)S(1)} %collective-permute-done.1, bf16[4,8,8,1536]{3,2,1,0:T(8,128)(2,1)S(1)} %bitcast.62, bf16[4,8,8,1536]{3,2,1,0:T(8,128)(2,1)S(1)} %multiply_convert_fusion, ...), kind=kLoop, calls=%fused_computation.19 | loop fusion | flops 84934656 | bytes 28311552 | tf_op jit(solution)/shard_map/concatenate | solution.py:20
  359.0 5.4 %fusion.28 = (bf16[1,2304,1536]{2,1,0:T(8,128)(2,1)}, bf16[1,2304,1536]{2,1,0:T(8,128)(2,1)}) fusion(bf16[1,2304,3072]{2,1,0:T(8,128)(2,1)S(1)} %bitcast.57), kind=kLoop, calls=%fused_computation.46 | loop fusion | bytes 28311552 | tf_op jit(solution)/shard_map/slice | solution.py:68
  364.4 10.2 %copy.24 = bf16[1,2304,1536]{1,2,0:T(8,128)(2,1)} copy(bf16[1,2304,1536]{2,1,0:T(8,128)(2,1)} %get-tuple-element.84) | data formatting | bytes 14155776
  374.5 9.9 %copy.25 = bf16[1,2304,1536]{1,2,0:T(8,128)(2,1)} copy(bf16[1,2304,1536]{2,1,0:T(8,128)(2,1)} %get-tuple-element.83) | data formatting | bytes 14155776
  384.5 78.7 %while.11 = (s32[]{:T(128)}, bf16[12,1,256,128]{2,3,0,1:T(8,128)(2,1)S(1)}, s32[12]{0:T(128)S(1)}, bf16[1,256,12,128]{1,3,2,0:T(8,128)(2,1)}, bf16[1,2304,12,128...) while((s32[]{:T(128)}, ...), condition=%wide.region_7.8_spmd.clone, body=%wide.region_4.7_spmd.clone.sunk | while | flops 306183680 | bytes 8666851 | solution.py:92
  387.2 1.7 fusion.41
  393.7 1.7 fusion.41
  400.3 1.7 fusion.41
  406.8 1.7 fusion.41
  413.4 1.7 fusion.41
  420.0 1.7 fusion.41
  426.5 1.7 fusion.41
  433.1 1.7 fusion.41
  439.6 1.7 fusion.41
  452.8 1.7 fusion.41
  463.3 4.6 fusion.22
  (130 shorter events, 50.6 us)
Async XLA Ops:
  6.5 3.8 copy-start
  6.5 4.5 copy-start.2
  6.5 129.5 %all-gather.3.cloned.1.call-start = ((), (), s32[]{:S(2)}) async-start(), calls=%async_computation | async-start | bytes 14598144 | tf_op jit(solution)/shard_map/all_gather | solution.py:47
  7.3 456.0 %all-gather.5.cloned.1.call-start = ((), (), s32[]{:S(2)}) async-start(), calls=%async_computation.1 | async-start | bytes 4866048 | tf_op jit(solution)/shard_map/all_gather | solution.py:94
  153.3 70.0 %collective-permute-start.1 = (bf16[4,8,8,3072]{3,2,1,0:T(8,128)(2,1)S(1)}, bf16[4,8,8,3072]{3,2,1,0:T(8,128)(2,1)S(1)}, u32[]{:S(2)}, u32[]{:S(2)}) collective-permute-start(bf16[4,8,8,3072]{3,2,1,0:T(8,128)(2,1)S(1)} %pad_maximum_fusion.2), channel_id=1, source_target_pairs={{32,0},{64,32},{96,64},{128,96},{160,128},{192,160},{224,192},{33,... | collective-permute-start | bytes 4718600 | tf_op jit(solution)/shard_map/ppermute | solution.py:19
  155.2 71.1 %collective-permute-start = (bf16[4,8,8,3072]{3,2,1,0:T(8,128)(2,1)S(1)}, bf16[4,8,8,3072]{3,2,1,0:T(8,128)(2,1)S(1)}, u32[]{:S(2)}, u32[]{:S(2)}) collective-permute-start(bf16[4,8,8,3072]{3,2,1,0:T(8,128)(2,1)S(1)} %pad_maximum_fusion.2), channel_id=1, source_target_pairs={{0,32},{32,64},{64,96},{96,128},{128,160},{160,192},{192,224},{1,3... | collective-permute-start | bytes 4718600 | tf_op jit(solution)/shard_map/ppermute | solution.py:18
  226.4 2.7 copy-start.3
  229.1 57.2 %collective-permute-start.3 = (bf16[4,24,8,3072]{3,2,1,0:T(8,128)(2,1)}, bf16[4,24,8,3072]{3,2,1,0:T(8,128)(2,1)}, u32[]{:S(2)}, u32[]{:S(2)}) collective-permute-start(bf16[4,24,8,3072]{3,2,1,0:T(8,128)(2,1)} %pad_maximum_fusion.1), channel_id=1, source_target_pairs={{1,0},{2,1},{3,2},{4,3},{5,4},{6,5},{7,6},{8,7},{9,8},{10,9},{11,1... | collective-permute-start | bytes 14155784 | tf_op jit(solution)/shard_map/ppermute | solution.py:19
  232.7 119.5 %collective-permute-start.2 = (bf16[4,24,8,3072]{3,2,1,0:T(8,128)(2,1)}, bf16[4,24,8,3072]{3,2,1,0:T(8,128)(2,1)}, u32[]{:S(2)}, u32[]{:S(2)}) collective-permute-start(bf16[4,24,8,3072]{3,2,1,0:T(8,128)(2,1)} %pad_maximum_fusion.1), channel_id=1, source_target_pairs={{0,1},{1,2},{2,3},{3,4},{4,5},{5,6},{6,7},{7,8},{8,9},{9,10},{10,1... | collective-permute-start | bytes 14155784 | tf_op jit(solution)/shard_map/ppermute | solution.py:18
  237.8 4.6 copy-start.5
  242.4 109.9 %copy-start.4 = (bf16[4,8,8,3072]{3,2,1,0:T(8,128)(2,1)S(1)}, bf16[4,8,8,3072]{3,2,1,0:T(8,128)(2,1)}, u32[]{:S(2)}) copy-start(bf16[4,8,8,3072]{3,2,1,0:T(8,128)(2,1)} %copy-done.3) | copy-start | bytes 4718596
  374.5 10.0 %copy-start.6 = (bf16[12,1,256,128]{2,3,0,1:T(8,128)(2,1)S(1)}, bf16[12,1,256,128]{2,3,0,1:T(8,128)(2,1)}, u32[]{:S(2)}) copy-start(bf16[12,1,256,128]{2,3,0,1:T(8,128)(2,1)} %custom-call) | copy-start | bytes 2359300
  384.5 78.8 %copy-start.7 = (f32[1536]{0:T(1024)S(1)}, f32[1536]{0:T(1024)}, u32[]{:S(2)}) copy-start(f32[1536]{0:T(1024)} %param.13) | copy-start | bytes 18436
  463.3 4.6 copy-start.1
Sparse Core Ops, SparseCore 0:
  10.1 125.8 all-gather.2
  234.8 133.5 all-gather.4
where the time goes:
time: 477 us; the launch traced here: 475 us
  waiting for transfers between devices  298 us (62%)
  matrix products  51.1 us (11%)
  local copies, waits for them, and re-layouts  45.3 us (9%)
  other arithmetic  30.5 us (6%)
  loops' own time  23.9 us (5%)
  between operations  13.6 us (3%)
  starting transfers between devices  12.3 us (3%)
    all_gather x1, waiting for transfers between devices, shards(): lax.all_gather(qkv_weight, 'wa', axis=0, tiled=True)  124 us
    ppermute x2, waiting for transfers between devices, padded(): after = lax.ppermute(initial, axis, down)  104 us
    ppermute x2, waiting for transfers between devices, padded(): before = lax.ppermute(last, axis, up)  69.1 us
    another operation x1, loops' own time, shards(): per_head = lax.map(one_head, jnp.arange(HEADS, dtype=jnp.int32))  23.9 us
    dot_general x12, matrix products, one_head(): jnp.einsum('nur,ncr->nuc', query_head_rows, key_head_rows, preferred_elem...  20.3 us
    unnamed x18, local copies, waits for them, and re-layouts  20.1 us
    dot_general x12, matrix products, one_head(): jnp.einsum('ypi,yif->ypf', probability_rows, value_head_rows, preferred_e...  19.1 us
    dot_general x2, matrix products, add_rows(): return jnp.dot(left, piece, preferred_element_type=jnp.float32)  11.7 us
  transfers between devices with their start and end apart: 6, of which 5 were waited for; matrix products, arithmetic and copies ran while one was open for 22% of the time, Pallas kernels for 0%

commit v1 on v0

--- a/solution.py
+++ b/solution.py
@@ -6,6 +6,14 @@
 HEADS = 12
 HD = 128
 TILE_T = 4
+
+
+def _push_task(mat):
+    views = []
+    for _ in range(lax.axis_size("wa")):
+        views.append(mat)
+    now = jnp.concatenate(lax.all_to_all(jnp.stack(views), "wa", 0, 0), 0)
+    return now
 
 
 def padded(x, sides, width):
@@ -44,7 +52,7 @@
     var = jnp.mean(centred * centred, axis=-1, keepdims=True)
     normed = centred / jnp.sqrt(var + 1e-06)
     modulated = (normed * (1.0 + scale) + shift).astype(jnp.bfloat16)
-    projected = add_rows(modulated, lax.all_gather(qkv_weight, "wa", axis=0, tiled=True))
+    projected = add_rows(modulated, _push_task(qkv_weight))
     query = per_head_norm(projected[:, :inner].reshape(count, HEADS, HD), q_gain)
     key = per_head_norm(projected[:, inner : 2 * inner].reshape(count, HEADS, HD), k_gain)
     value = projected[:, 2 * inner :].astype(jnp.bfloat16)

time: 477 us -> 676 us (1.42)
  waiting for transfers between devices: 298 us -> 479 us
  starting transfers between devices: 12.3 us -> 23 us
  local copies, waits for them, and re-layouts: 45.3 us -> 52.8 us
    all_to_all x0 -> x1, waiting for transfers between devices: none -> 304 us  [_push_task(): now = jnp.concatenate(lax.all_to_all(jnp.stack(views), 'wa', 0, 0), 0)]
    all_gather x1 -> x0, waiting for transfers between devices: 124 us -> none  [shards(): lax.all_gather(qkv_weight, 'wa', axis=0, tiled=True)]
    all_to_all x0 -> x1, starting transfers between devices: none -> 11.8 us  [_push_task(): now = jnp.concatenate(lax.all_to_all(jnp.stack(views), 'wa', 0, 0), 0)]
    another operation x0 -> x1, local copies, waits for them, and re-layouts: none -> 7.75 us  [_push_task(): now = jnp.concatenate(lax.all_to_all(jnp.stack(views), 'wa', 0, 0), 0)]
    unnamed x18 -> x22, local copies, waits for them, and re-layouts: 20.1 us -> 20.1 us
  transfers between devices with their start and end apart: 6 -> 6, of which waited for: 5 -> 5; matrix products, arithmetic and copies ran while one was open for 22% -> 15% of each run, Pallas kernels for 0% -> 0%
where the time goes in v1:
time: 676 us; the launch traced here: 670 us
  waiting for transfers between devices  479 us (71%)
  local copies, waits for them, and re-layouts  52.8 us (8%)
  matrix products  51.1 us (8%)
  other arithmetic  26.9 us (4%)
  loops' own time  23.9 us (4%)
  starting transfers between devices  23 us (3%)
  between operations  13.6 us (2%)
    all_to_all x1, waiting for transfers between devices, _push_task(): now = jnp.concatenate(lax.all_to_all(jnp.stack(views), 'wa', 0, 0), 0)  304 us
    ppermute x2, waiting for transfers between devices, padded(): after = lax.ppermute(initial, axis, down)  104 us
    ppermute x2, waiting for transfers between devices, padded(): before = lax.ppermute(last, axis, up)  71.2 us
    another operation x1, loops' own time, shards(): per_head = lax.map(one_head, jnp.arange(HEADS, dtype=jnp.int32))  23.9 us
    dot_general x12, matrix products, one_head(): jnp.einsum('nur,ncr->nuc', query_head_rows, key_head_rows, preferred_elem...  20.4 us
    unnamed x22, local copies, waits for them, and re-layouts  20.1 us
    dot_general x12, matrix products, one_head(): jnp.einsum('ypi,yif->ypf', probability_rows, value_head_rows, preferred_e...  19.1 us
  transfers between devices with their start and end apart: 6, of which 5 were waited for; matrix products, arithmetic and copies ran while one was open for 15% of the time, Pallas kernels for 0%

profile of v1, /device:TPU:28, one launch (start us, length us, event | category | flops | bytes accessed | tf_op | source)
XLA Modules:
  0.0 670.4 jit_solution(3884243082450404027)
XLA Ops:
  6.5 7.8 %stack.2 = bf16[32,48,4608]{2,1,0:T(8,128)(2,1)} broadcast(bf16[48,4608]{1,0:T(8,128)(2,1)} %param.14), dimensions={1,2} | broadcast | bytes 14598144 | tf_op jit(solution)/shard_map/stack | solution.py:15
  14.3 11.8 %all-to-all-start = ((bf16[32,48,4608]{2,1,0:T(8,128)(2,1)}), bf16[32,48,4608]{2,1,0:T(8,128)(2,1)}, u32[]{:S(2)}, u32[]{:S(2)}) async-start(bf16[32,48,4608]{2,1,0:T(8,128)(2,1)} %stack.2), calls=%async_computation | async-start | bytes 28311552 | tf_op jit(solution)/shard_map/all_to_all | solution.py:15
  27.1 304.0 %all-to-all-done = bf16[32,48,4608]{2,1,0:T(8,128)(2,1)} async-done(((bf16[32,48,4608]{2,1,0:T(8,128)(2,1)}), bf16[32,48,4608]{2,1,0:T(8,128)(2,1)}, u32[]{:S(2)}, u32[]{:S(2)}) %all-to-all-start) | async-done | bytes 14155808 | tf_op jit(solution)/shard_map/all_to_all | solution.py:15
  331.1 7.0 %fusion.31 = f32[256,4608]{1,0:T(8,128)S(1)} fusion(bf16[256,1536]{1,0:T(8,128)(2,1)S(1)} %bitcast.59, bf16[1536,4608]{1,0:T(8,128)(2,1)} %bitcast.1), kind=kOutput, calls=%fused_computation.48 | convolution fusion | flops 3623878656 | bytes 19660800 | tf_op jit(solution)/shard_map/dot_general | solution.py:33
  338.1 2.5 slice_multiply_fusion
  346.0 2.2 multiply_convert_fusion
  348.4 2.7 collective-permute-start.1
  351.0 4.1 collective-permute-start
  355.1 63.4 %collective-permute-done.1 = bf16[4,8,8,3072]{3,2,1,0:T(8,128)(2,1)S(1)} collective-permute-done((bf16[4,8,8,3072]{3,2,1,0:T(8,128)(2,1)S(1)}, bf16[4,8,8,3072]{3,2,1,0:T(8,128)(2,1)S(1)}, u32[]{:S(2)}, u32[]{:S(2)}) %collective-permute-start.1) | collective-permute-done | bytes 1572896 | tf_op jit(solution)/shard_map/ppermute | solution.py:27
  418.5 2.6 collective-permute-done
  421.2 2.7 pad_maximum_fusion.1
  423.9 1.9 collective-permute-start.3
  425.8 2.6 collective-permute-start.2
  428.5 3.0 copy.9
  431.6 3.0 copy.10
  436.2 2.7 multiply_convert_fusion.1
  438.9 40.4 %collective-permute-done.3 = bf16[4,24,8,3072]{3,2,1,0:T(8,128)(2,1)} collective-permute-done((bf16[4,24,8,3072]{3,2,1,0:T(8,128)(2,1)}, bf16[4,24,8,3072]{3,2,1,0:T(8,128)(2,1)}, u32[]{:S(2)}, u32[]{:S(2)}) %collective-permute-start.3) | collective-permute-done | bytes 4718624 | tf_op jit(solution)/shard_map/ppermute | solution.py:27
  479.3 68.5 %collective-permute-done.2 = bf16[4,24,8,3072]{3,2,1,0:T(8,128)(2,1)} collective-permute-done((bf16[4,24,8,3072]{3,2,1,0:T(8,128)(2,1)}, bf16[4,24,8,3072]{3,2,1,0:T(8,128)(2,1)}, u32[]{:S(2)}, u32[]{:S(2)}) %collective-permute-start.2) | collective-permute-done | bytes 4718624 | tf_op jit(solution)/shard_map/ppermute | solution.py:26
  547.9 6.9 %pad_maximum_fusion = bf16[4,24,24,3072]{3,2,1,0:T(8,128)(2,1)S(1)} fusion(bf16[4,24,8,3072]{3,2,1,0:T(8,128)(2,1)} %collective-permute-done.3, bf16[4,8,8,3072]{3,2,1,0:T(8,128)(2,1)S(1)} %collective-permute-done.1, bf16[4,8,8,1536]{3,2,1,0:T(8,128)(2,1)S(1)} %bitcast.54, bf16[4,8,8,1536]{3,2,1,0:T(8,128)(2,1)S(1)} %multiply_convert_fusion, ...), kind=kLoop, calls=%fused_computation.19 | loop fusion | flops 84934656 | bytes 28311552 | tf_op jit(solution)/shard_map/concatenate | solution.py:28
  554.7 5.4 fusion.30
  560.2 9.7 %copy.24 = bf16[1,2304,1536]{1,2,0:T(8,128)(2,1)} copy(bf16[1,2304,1536]{2,1,0:T(8,128)(2,1)} %get-tuple-element.84) | data formatting | bytes 14155776
  569.9 10.3 %copy.25 = bf16[1,2304,1536]{1,2,0:T(8,128)(2,1)} copy(bf16[1,2304,1536]{2,1,0:T(8,128)(2,1)} %get-tuple-element.83) | data formatting | bytes 14155776
  580.2 78.7 %while.11 = (s32[]{:T(128)}, bf16[12,1,256,128]{2,3,0,1:T(8,128)(2,1)S(1)}, s32[12]{0:T(128)S(1)}, bf16[1,256,12,128]{1,3,2,0:T(8,128)(2,1)}, bf16[1,2304,12,128...) while((s32[]{:T(128)}, ...), condition=%wide.region_7.8_spmd.clone, body=%wide.region_4.7_spmd.clone.sunk | while | flops 306183680 | bytes 8666851 | solution.py:100
  582.9 1.7 fusion.43
  589.4 1.7 fusion.43
  596.0 1.7 fusion.43
  602.5 1.7 fusion.43
  609.1 1.7 fusion.43
  622.2 1.7 fusion.43
  635.3 1.7 fusion.43
  648.5 1.7 fusion.43
  659.0 4.6 fusion.22
  (132 shorter events, 49.5 us)
Async XLA Ops:
  6.5 20.1 %copy-start = (f32[128]{0:T(128)S(1)}, f32[128]{0:T(128)}, u32[]{:S(2)}) copy-start(f32[128]{0:T(128)} %param.17) | copy-start | bytes 1540
  14.3 11.8 %copy-start.2 = (bf16[4,8,8,1536]{3,2,1,0:T(8,128)(2,1)S(1)}, bf16[4,8,8,1536]{3,2,1,0:T(8,128)(2,1)}, u32[]{:S(2)}) copy-start(bf16[4,8,8,1536]{3,2,1,0:T(8,128)(2,1)} %param.10) | copy-start | bytes 2359300
  14.3 12.4 %copy-start.6 = (f32[1536]{0:T(1024)S(1)}, f32[1536]{0:T(1024)}, u32[]{:S(2)}) copy-start(f32[1536]{0:T(1024)} %param.12) | copy-start | bytes 18436
  14.3 12.4 %copy-start.5 = (f32[1536]{0:T(1024)S(1)}, f32[1536]{0:T(1024)}, u32[]{:S(2)}) copy-start(f32[1536]{0:T(1024)} %param.11) | copy-start | bytes 18436
  14.3 316.8 %all-to-all-start = ((bf16[32,48,4608]{2,1,0:T(8,128)(2,1)}), bf16[32,48,4608]{2,1,0:T(8,128)(2,1)}, u32[]{:S(2)}, u32[]{:S(2)}) async-start(bf16[32,48,4608]{2,1,0:T(8,128)(2,1)} %stack.2), calls=%async_computation | async-start | bytes 28311552 | tf_op jit(solution)/shard_map/all_to_all | solution.py:15
  26.1 632.9 %all-gather.2.cloned.1.call-start = ((), (), s32[]{:S(2)}) async-start(), calls=%async_computation.1 | async-start | bytes 4866048 | tf_op jit(solution)/shard_map/all_gather | solution.py:102
  348.4 70.2 %collective-permute-start.1 = (bf16[4,8,8,3072]{3,2,1,0:T(8,128)(2,1)S(1)}, bf16[4,8,8,3072]{3,2,1,0:T(8,128)(2,1)S(1)}, u32[]{:S(2)}, u32[]{:S(2)}) collective-permute-start(bf16[4,8,8,3072]{3,2,1,0:T(8,128)(2,1)S(1)} %pad_maximum_fusion.2), channel_id=1, source_target_pairs={{32,0},{64,32},{96,64},{128,96},{160,128},{192,160},{224,192},{33,... | collective-permute-start | bytes 4718600 | tf_op jit(solution)/shard_map/ppermute | solution.py:27
  351.0 70.2 %collective-permute-start = (bf16[4,8,8,3072]{3,2,1,0:T(8,128)(2,1)S(1)}, bf16[4,8,8,3072]{3,2,1,0:T(8,128)(2,1)S(1)}, u32[]{:S(2)}, u32[]{:S(2)}) collective-permute-start(bf16[4,8,8,3072]{3,2,1,0:T(8,128)(2,1)S(1)} %pad_maximum_fusion.2), channel_id=1, source_target_pairs={{0,32},{32,64},{64,96},{96,128},{128,160},{160,192},{192,224},{1,3... | collective-permute-start | bytes 4718600 | tf_op jit(solution)/shard_map/ppermute | solution.py:26
  421.2 2.7 copy-start.3
  423.9 55.4 %collective-permute-start.3 = (bf16[4,24,8,3072]{3,2,1,0:T(8,128)(2,1)}, bf16[4,24,8,3072]{3,2,1,0:T(8,128)(2,1)}, u32[]{:S(2)}, u32[]{:S(2)}) collective-permute-start(bf16[4,24,8,3072]{3,2,1,0:T(8,128)(2,1)} %pad_maximum_fusion.1), channel_id=1, source_target_pairs={{1,0},{2,1},{3,2},{4,3},{5,4},{6,5},{7,6},{8,7},{9,8},{10,9},{11,1... | collective-permute-start | bytes 14155784 | tf_op jit(solution)/shard_map/ppermute | solution.py:27
  425.8 122.0 %collective-permute-start.2 = (bf16[4,24,8,3072]{3,2,1,0:T(8,128)(2,1)}, bf16[4,24,8,3072]{3,2,1,0:T(8,128)(2,1)}, u32[]{:S(2)}, u32[]{:S(2)}) collective-permute-start(bf16[4,24,8,3072]{3,2,1,0:T(8,128)(2,1)} %pad_maximum_fusion.1), channel_id=1, source_target_pairs={{0,1},{1,2},{2,3},{3,4},{4,5},{5,6},{6,7},{7,8},{8,9},{9,10},{10,1... | collective-permute-start | bytes 14155784 | tf_op jit(solution)/shard_map/ppermute | solution.py:26
  431.6 4.6 copy-start.7
  436.1 111.7 %copy-start.4 = (bf16[4,8,8,3072]{3,2,1,0:T(8,128)(2,1)S(1)}, bf16[4,8,8,3072]{3,2,1,0:T(8,128)(2,1)}, u32[]{:S(2)}) copy-start(bf16[4,8,8,3072]{3,2,1,0:T(8,128)(2,1)} %copy-done.3) | copy-start | bytes 4718596
  569.8 10.3 %copy-start.8 = (bf16[12,1,256,128]{2,3,0,1:T(8,128)(2,1)S(1)}, bf16[12,1,256,128]{2,3,0,1:T(8,128)(2,1)}, u32[]{:S(2)}) copy-start(bf16[12,1,256,128]{2,3,0,1:T(8,128)(2,1)} %custom-call) | copy-start | bytes 2359300
  580.2 78.8 %copy-start.9 = (f32[1536]{0:T(1024)S(1)}, f32[1536]{0:T(1024)}, u32[]{:S(2)}) copy-start(f32[1536]{0:T(1024)} %param.13) | copy-start | bytes 18436
  659.0 4.6 copy-start.1
Sparse Core Ops, SparseCore 0:
  428.6 137.5 all-gather.1
